TPU v7x, 512 devices: a whole 4x4x16 slice. The times are simulated.
512 devices in a mesh: ctx: 256 (over y, x, z), kv: 2 (over core).
Axes of the slice: x: 4, y: 4, z: 16, core: 2. Of those that a mesh axis runs over, the one named last changes fastest.
Arguments:
- stretch_q: bfloat16 [32768, 5120], P('ctx', 'kv'), may hold values from -40 to 40
- stretch_do: bfloat16 [32768, 5120], P('ctx', 'kv'), may hold values from -24 to 24
- stretch_out: bfloat16 [32768, 5120], P('ctx', 'kv'), may hold values from -6 to 6
- stretch_lse: float32 [32768, 40], P('ctx', 'kv'), may hold values from -60 to 60, as said below
- stretch_pk: bfloat16 [128, 1024], P(None, 'kv'), may hold values from -20 to 20
- stretch_pv: bfloat16 [128, 1024], P(None, 'kv'), may hold values from -6 to 6
- global_q: bfloat16 [32768, 5120], P('ctx', 'kv'), may hold values from -40 to 40
- global_do: bfloat16 [32768, 5120], P('ctx', 'kv'), may hold values from -24 to 24
- global_out: bfloat16 [32768, 5120], P('ctx', 'kv'), may hold values from -6 to 6
- global_lse: float32 [32768, 40], P('ctx', 'kv'), may hold values from -60 to 60, as said below
- global_pk: bfloat16 [128, 1024], P(None, 'kv'), may hold values from -20 to 20
- global_pv: bfloat16 [128, 1024], P(None, 'kv'), may hold values from -6 to 6
- wq_stretch: bfloat16 [5120, 5120], P('ctx', 'kv'), may hold values from -0.5 to 0.5
- wk_stretch: bfloat16 [5120, 1024], P('ctx', 'kv'), may hold values from -0.5 to 0.5
- wv_stretch: bfloat16 [5120, 1024], P('ctx', 'kv'), may hold values from -0.5 to 0.5
- wq_global: bfloat16 [5120, 5120], P('ctx', 'kv'), may hold values from -0.5 to 0.5
- wk_global: bfloat16 [5120, 1024], P('ctx', 'kv'), may hold values from -0.5 to 0.5
- wv_global: bfloat16 [5120, 1024], P('ctx', 'kv'), may hold values from -0.5 to 0.5
Outputs:
- prompt_grad: float32 [128, 5120], P(None, 'ctx')
Inputs may be any that keep to these rules, and one draw needn't show every extreme that they name: `stretch_lse`: saved log totals of the stretched layer: each at least the log of the sum of exp of its allowed prompt scores. `global_lse`: saved log totals of the global layer: each at least the log of the sum of exp of its allowed prompt scores.
All inputs are finite; a program needn't handle non-finite values.
Results may differ from a plain program's by a relative error of at most 0.0041.
Values may be sent and summed in bfloat16 or wider, within the bound.
A program may use at most 64 MiB of HBM per device.

v0:
```python
import jax
import jax.numpy as jnp
from jax import lax
from jax.sharding import PartitionSpec as P

HD = 128
HPG = 5


NEG = -1e30


def local_terms(queries, cotangent, saved_out, log_total, prompt_k, prompt_v, offset, span):
    tokens = queries.shape[0]
    groups = prompt_k.shape[1] // HD
    prompt_len = prompt_k.shape[0]
    inv_root = HD ** (-0.5)
    query_heads = queries.reshape(tokens, groups, HPG, HD)
    grad_out = cotangent.reshape(tokens, groups, HPG, HD)
    out_heads = saved_out.reshape(tokens, groups, HPG, HD)
    totals = jnp.transpose(log_total.reshape(tokens, groups, HPG), (1, 2, 0))
    key_heads = prompt_k.reshape(prompt_len, groups, HD)
    value_heads = prompt_v.reshape(prompt_len, groups, HD)
    scores = (
        jnp.einsum("qghd,pgd->ghqp", query_heads, key_heads, preferred_element_type=jnp.float32)
        * inv_root
    )
    qpos = offset + jnp.arange(tokens)
    ppos = jnp.arange(prompt_len)
    allowed = (ppos[None, :] <= qpos[:, None]) & (qpos[:, None] < span)
    probs = jnp.exp(jnp.where(allowed, scores - totals[..., None], NEG))
    row_delta = jnp.einsum(
        "qghd,qghd->ghq", grad_out, out_heads, preferred_element_type=jnp.float32
    )
    grad_prob = jnp.einsum(
        "qghd,pgd->ghqp", grad_out, value_heads, preferred_element_type=jnp.float32
    )
    grad_score = (probs * (grad_prob - row_delta[..., None])).astype(jnp.bfloat16)
    grad_k = (
        jnp.einsum("ghqp,qghd->pgd", grad_score, query_heads, preferred_element_type=jnp.float32)
        * inv_root
    )
    grad_v = jnp.einsum(
        "ghqp,qghd->pgd", probs.astype(jnp.bfloat16), grad_out, preferred_element_type=jnp.float32
    )

    def query_side():
        rows = (
            jnp.einsum("ghqp,pgd->qghd", grad_score, key_heads, preferred_element_type=jnp.float32)
            * inv_root
        )
        return rows.reshape(tokens, groups * HPG * HD)

    def no_rows():
        return jnp.zeros((tokens, groups * HPG * HD), jnp.float32)

    grad_rows = lax.cond(offset < prompt_len, query_side, no_rows)
    return (
        grad_rows,
        grad_k.reshape(prompt_len, groups * HD),
        grad_v.reshape(prompt_len, groups * HD),
    )


def place_rows(rows, offset, prompt_len):
    tokens, width = rows.shape
    padded = jnp.zeros((prompt_len + tokens, width), jnp.float32)
    padded = lax.dynamic_update_slice(padded, rows, (jnp.minimum(offset, prompt_len), 0))
    return padded[:prompt_len]


def project(grads, weights):
    result = None
    for grad_part, weight in zip(grads, weights):
        term = jnp.einsum("pf,cf->pc", grad_part, weight, preferred_element_type=jnp.float32)
        result = term if result is None else result + term
    return result


def local(
    stretch_q,
    stretch_do,
    stretch_out,
    stretch_lse,
    stretch_pk,
    stretch_pv,
    global_q,
    global_do,
    global_out,
    global_lse,
    global_pk,
    global_pv,
    wq_stretch,
    wk_stretch,
    wv_stretch,
    wq_global,
    wk_global,
    wv_global,
):
    tokens = stretch_q.shape[0]
    prompt_len = stretch_pk.shape[0]
    sequence = tokens * lax.axis_size("ctx")
    stretch_span = min(8192, sequence // 4)
    offset = lax.axis_index("ctx") * tokens

    def stretch_side():
        return local_terms(
            stretch_q,
            stretch_do,
            stretch_out,
            stretch_lse,
            stretch_pk,
            stretch_pv,
            offset,
            stretch_span,
        )

    def stretch_empty():
        return (
            jnp.zeros((tokens, stretch_q.shape[1]), jnp.float32),
            jnp.zeros((stretch_pk.shape[0], stretch_pk.shape[1]), jnp.float32),
            jnp.zeros((stretch_pv.shape[0], stretch_pv.shape[1]), jnp.float32),
        )

    stretch_terms = lax.cond(offset < stretch_span, stretch_side, stretch_empty)
    global_terms = local_terms(
        global_q, global_do, global_out, global_lse, global_pk, global_pv, offset, sequence
    )
    key_totals = lax.psum(
        (stretch_terms[1], stretch_terms[2], global_terms[1], global_terms[2]), "ctx"
    )
    query_totals = lax.psum(
        (
            place_rows(stretch_terms[0], offset, prompt_len),
            place_rows(global_terms[0], offset, prompt_len),
        ),
        "ctx",
    )
    query_grads = (query_totals[0].astype(jnp.bfloat16), query_totals[1].astype(jnp.bfloat16))
    key_bf = [part.astype(jnp.bfloat16) for part in key_totals]
    partial_grad = project(
        (query_grads[0], key_bf[0], key_bf[1]), (wq_stretch, wk_stretch, wv_stretch)
    )
    partial_grad = partial_grad + project(
        (query_grads[1], key_bf[2], key_bf[3]), (wq_global, wk_global, wv_global)
    )
    return lax.psum(partial_grad, "kv")


def solution(mesh):
    return jax.shard_map(
        local,
        mesh=mesh,
        in_specs=(
            P("ctx", "kv"),
            P("ctx", "kv"),
            P("ctx", "kv"),
            P("ctx", "kv"),
            P(None, "kv"),
            P(None, "kv"),
            P("ctx", "kv"),
            P("ctx", "kv"),
            P("ctx", "kv"),
            P("ctx", "kv"),
            P(None, "kv"),
            P(None, "kv"),
            P("ctx", "kv"),
            P("ctx", "kv"),
            P("ctx", "kv"),
            P("ctx", "kv"),
            P("ctx", "kv"),
            P("ctx", "kv"),
        ),
        out_specs=P(None, "ctx"),
        check_vma=False,
    )
```

profile of v0, /device:TPU:1, one launch (start us, length us, event | category | flops | bytes accessed | tf_op | source)
XLA Modules:
  0.0 1450.8 jit_solution(12538708939189607843)
XLA Ops:
  0.0 0.0 copy-start
  0.0 0.0 copy-start.2
  0.1 0.8 reshape.76
  0.8 1.0 copy.56
  1.9 0.9 reshape.77
  2.8 0.0 copy-start.3
  2.8 1.5 copy.60
  4.3 0.0 copy-done.2
  4.3 0.3 copy.57
  4.6 0.0 copy-done.3
  4.6 0.3 copy.112
  5.0 0.2 fusion.22
  5.2 0.5 fusion.18
  5.7 0.4 fusion.25
  6.0 0.3 fusion.21
  6.4 1.1 fusion.23
  7.5 0.0 copy-start.4
  7.5 0.0 copy-start.6
  7.5 0.0 copy-start.12
  7.5 0.3 conditional.4
  7.5 0.3 convolution_multiply_fusion.1
  7.8 0.7 copy-done.4
  8.5 0.0 copy-done.5
  8.6 0.0 copy-done.6
  8.6 0.0 copy-done.12
  8.6 0.0 copy-start.1
  8.6 1.1 copy-done.1
  9.7 6.6 conditional.3
  9.7 0.1 copy.52
  9.9 0.3 copy.54
  10.2 1.4 copy.105
  11.6 0.2 fusion.9
  11.9 1.4 copy.53
  13.3 0.5 fusion.5
  13.7 0.4 fusion.11
  14.1 0.3 fusion.8
  14.4 0.4 fusion.10
  14.8 1.4 conditional
  14.8 1.4 convolution_multiply_fusion
  16.2 0.2 broadcast.76.clone
  16.4 10.6 dynamic_update_slice.6
  27.0 1.1 slice.8
  28.1 0.2 broadcast.76.clone.1
  28.3 10.6 dynamic_update_slice.7
  38.9 1.2 slice.9
  40.0 0.0 copy-start.9
  40.0 0.0 copy-start.10
  40.0 0.0 copy-start.7
  40.0 1187.1 %all-reduce.2 = (bf16[128,2560]{0,1:T(8,128)(2,1)S(1)}, bf16[128,512]{0,1:T(8,128)(2,1)S(1)}, bf16[128,512]{0,1:T(8,128)(2,1)S(1)}, bf16[128,2560]{0,1:T(8,128)(...) all-reduce(f32[128,2560]{0,1:T(8,128)} %slice.8, ...), channel_id=1, replica_groups=mesh['ctx'=256,'kv'=2] {'ctx'}, use_global_device_ids=true, to_apply=%region_4.5 | all-reduce | flops 917504 | bytes 5505024 | tf_op jit(solution)/shard_map/psum | solution.py:132
  1227.2 0.0 copy-start.11
  1227.2 0.0 copy-start.8
  1227.2 0.0 copy-done
  1227.2 0.2 fusion.38
  1227.4 0.0 copy-done.9
  1227.4 0.1 convolution_add_fusion.3
  1227.6 0.0 copy-done.10
  1227.6 0.1 convolution_add_fusion.2
  1227.7 0.0 copy-done.7
  1227.7 0.2 fusion.37
  1227.9 0.0 copy-done.11
  1228.0 0.1 convolution_add_fusion.1
  1228.1 0.0 copy-done.8
  1228.1 0.1 fusion.24
  1228.2 222.6 %psum.55 = f32[128,20]{0,1:T(8,128)} all-reduce(f32[128,20]{0,1:T(8,128)S(1)} %fusion.24), channel_id=1, replica_groups=mesh['ctx'=256,'kv'=2] {'kv'}, use_global_device_ids=true, to_apply=%region_12.13 | all-reduce | flops 2560 | bytes 20480 | tf_op jit(solution)/shard_map/psum | solution.py:147
  (9 shorter events, 0.1 us)
Async XLA Ops:
  0.0 1227.2 %copy-start = (bf16[20,2560]{1,0:T(8,128)(2,1)S(1)}, bf16[20,2560]{1,0:T(8,128)(2,1)}, u32[]{:S(2)}) copy-start(bf16[20,2560]{1,0:T(8,128)(2,1)} %param.36) | copy-start | bytes 307204
  0.0 4.3 copy-start.2
  2.8 1.8 copy-start.3
  7.5 1.1 copy-start.4
  7.5 1.1 copy-start.5
  7.5 1.1 copy-start.6
  7.5 1.1 copy-start.12
  8.6 1.1 copy-start.1
  40.0 1187.4 %copy-start.9 = (bf16[20,512]{1,0:T(8,128)(2,1)S(1)}, bf16[20,512]{1,0:T(8,128)(2,1)}, u32[]{:S(2)}) copy-start(bf16[20,512]{1,0:T(8,128)(2,1)} %param.37) | copy-start | bytes 61444
  40.0 1187.5 %copy-start.10 = (bf16[20,512]{1,0:T(8,128)(2,1)S(1)}, bf16[20,512]{1,0:T(8,128)(2,1)}, u32[]{:S(2)}) copy-start(bf16[20,512]{1,0:T(8,128)(2,1)} %param.38) | copy-start | bytes 61444
  40.0 1187.7 %copy-start.7 = (bf16[20,2560]{1,0:T(8,128)(2,1)S(1)}, bf16[20,2560]{1,0:T(8,128)(2,1)}, u32[]{:S(2)}) copy-start(bf16[20,2560]{1,0:T(8,128)(2,1)} %param.39) | copy-start | bytes 307204
  1227.2 0.7 copy-start.11
  1227.2 0.9 copy-start.8
where the time goes:
time: 1450 us
  blocking collectives  1410 us (97%)
  local copies, waits for them, and re-layouts  33.8 us (2%)
    psum x1, blocking collectives, local(): lax.psum((place_rows(stretch_terms[0], offset, prompt_len), place_rows(gl...  1190 us
    psum x1, blocking collectives, local(): return lax.psum(partial_grad, 'kv')  223 us

commit v1 on v0

v1 whole, which is shorter than its diff:
```python
import functools

import jax
import jax.numpy as jnp
from jax import lax
from jax.experimental import pallas as pl
from jax.experimental.pallas import tpu as pltpu
from jax.sharding import PartitionSpec as P

HD = 128
HPG = 5
NEG = -1e30
PLANE = 16
MESH = pl.DeviceIdType.MESH
F32 = jnp.float32
BF16 = jnp.bfloat16


def nt(a, b):
    return lax.dot_general(a, b, (((1,), (1,)), ((), ())), preferred_element_type=F32)


def nn(a, b):
    return lax.dot_general(a, b, (((1,), (0,)), ((), ())), preferred_element_type=F32)


def unit_of(p):
    parity = (p % 4 + p // 4) % 2
    return p // 2 + 8 * (1 - parity)


def body(
    zs,
    sq, sdo, sout, slse, spk, spv,
    gq, gdo, gout, glse, gpk, gpv,
    wqs, wks, wvs, wqg, wkg, wvg,
    o_ref,
    q_buf, do_buf, out_buf, lse_buf, lse_t, pk_buf, pv_buf,
    w_kv, w_q, rw_kv, rw_q, wp,
    part, r_kv, s_buf, r_z,
    q_units, r_q, g_buf,
    o_send, r_o, half, r_half,
    load_sem, send_sem, recv_sem,
):
    me = lax.axis_index("ctx")
    kv = lax.axis_index("kv")
    pid = me // zs
    z = me % zs
    groups = pk_buf.shape[2] // HD
    tokens = q_buf.shape[1]
    width = groups * HPG * HD
    inv_root = HD ** (-0.5)
    near = pid < 4
    wide = pid < 8

    def plane_dev(p):
        return (p * zs + z, kv)

    def z_dev(zz):
        return (pid * zs + zz, kv)

    def send(src, dst, phase, dev):
        pltpu.make_async_remote_copy(
            src_ref=src, dst_ref=dst, send_sem=send_sem.at[phase], recv_sem=recv_sem.at[phase],
            device_id=dev, device_id_type=MESH,
        ).start()

    def wait_recv(ref, phase):
        pltpu.make_async_copy(ref, ref, recv_sem.at[phase]).wait()

    def wait_send(ref, phase):
        pltpu.make_async_copy(ref, ref, send_sem.at[phase]).wait()

    w_loads = []
    w_srcs = (
        (wks, w_kv, 0, 512), (wvs, w_kv, 512, 512), (wkg, w_kv, 1024, 512), (wvg, w_kv, 1536, 512),
        (wqs, w_q, 0, width), (wqg, w_q, width, width),
    )
    for n, (src, dst, start, size) in enumerate(w_srcs):
        w_loads.append(pltpu.make_async_copy(src, dst.at[:, pl.ds(start, size)], load_sem.at[n]))
    layer_loads = []
    for layer, srcs in enumerate(((sq, sdo, sout, slse, spk, spv), (gq, gdo, gout, glse, gpk, gpv))):
        dsts = (q_buf, do_buf, out_buf, lse_buf, pk_buf, pv_buf)
        layer_loads.append([
            pltpu.make_async_copy(s, d.at[layer], load_sem.at[6 + 6 * layer + n])
            for n, (s, d) in enumerate(zip(srcs, dsts))
        ])
    for c in w_loads:
        c.start()
    for c in layer_loads[1]:
        c.start()

    @pl.when(near)
    def _():
        for c in layer_loads[0]:
            c.start()

    barrier = pltpu.get_barrier_semaphore()

    @pl.loop(1, PLANE)
    def _(k):
        pl.semaphore_signal(barrier, inc=1, device_id=plane_dev((pid + k) % PLANE), device_id_type=MESH)

    @pl.loop(1, zs)
    def _(k):
        pl.semaphore_signal(barrier, inc=1, device_id=z_dev((z + k) % zs), device_id_type=MESH)

    pl.semaphore_signal(barrier, inc=1, device_id=(me, 1 - kv), device_id_type=MESH)

    wp[...] = jnp.zeros_like(wp)

    @pl.when(jnp.logical_not(wide))
    def _():
        g_buf[:, :, 384:512] = jnp.zeros((zs, 8, HD), BF16)

    for c in w_loads:
        c.wait()
    pl.semaphore_wait(barrier, (PLANE - 1) + (zs - 1) + 1)

    def q_start(p):
        return pl.multiple_of(jnp.where(p < 8, 384 * p, 3072 + 256 * (p - 8)), HD)

    @pl.loop(1, PLANE)
    def _(k):
        p = (pid + k) % PLANE
        u = unit_of(p)
        send(w_kv.at[:, pl.ds(pl.multiple_of(u * HD, HD), HD)], rw_kv.at[pid], 0, plane_dev(p))

        @pl.when(p < 8)
        def _():
            send(w_q.at[:, pl.ds(q_start(p), 384)], rw_q.at[pid], 1, plane_dev(p))

        @pl.when(p >= 8)
        def _():
            send(w_q.at[:, pl.ds(q_start(p), 256)], rw_q.at[pid, :, pl.ds(0, 256)], 1, plane_dev(p))

    def layer_terms(layer):
        for c in layer_loads[layer]:
            c.wait()
        pad = jnp.zeros((tokens, HD - groups * HPG), F32)
        lse_t[layer] = jnp.transpose(jnp.concatenate([lse_buf[layer], pad], axis=1))
        rows = lax.broadcasted_iota(jnp.int32, (HD, tokens), 0)
        cols = lax.broadcasted_iota(jnp.int32, (HD, tokens), 1) + me * tokens
        allowed = rows <= cols
        ones = jnp.ones((16, 2 * HD), BF16)
        for g in range(groups):
            heads = [pl.ds((g * HPG + h) * HD, HD) for h in range(HPG)]
            q_cat = jnp.concatenate([q_buf[layer, :, s] for s in heads], axis=0)
            do_cat = jnp.concatenate([do_buf[layer, :, s] for s in heads], axis=0)
            out_cat = jnp.concatenate([out_buf[layer, :, s] for s in heads], axis=0)
            key = pk_buf[layer, :, g * HD:(g + 1) * HD]
            val = pv_buf[layer, :, g * HD:(g + 1) * HD]
            prod = do_cat.astype(F32) * out_cat.astype(F32)
            high = prod.astype(BF16)
            low = (prod - high.astype(F32)).astype(BF16)
            delta = nt(ones, jnp.concatenate([high, low], axis=1))
            scores = nt(key, q_cat)
            grad_prob = nt(val, do_cat)
            p_parts, ds_parts = [], []
            for h in range(HPG):
                cut = slice(h * tokens, (h + 1) * tokens)
                row = g * HPG + h
                arg = scores[:, cut] * inv_root - lse_t[layer, row:row + 1, :]
                probs = jnp.exp(jnp.where(allowed, arg, NEG))
                p_parts.append(probs.astype(BF16))
                ds_parts.append((probs * (grad_prob[:, cut] - delta[0:1, cut])).astype(BF16))
            p_cat = jnp.concatenate(p_parts, axis=1)
            ds_cat = jnp.concatenate(ds_parts, axis=1)
            part[8 * layer + g] = (nn(ds_cat, q_cat) * inv_root).astype(BF16)
            part[8 * layer + 4 + g] = nn(p_cat, do_cat).astype(BF16)

            @pl.when(me == 0)
            def _():
                key_t = jnp.transpose(key.astype(F32)).astype(BF16)
                rows_t = nn(key_t, ds_cat) * inv_root
                q_units[:, pl.ds(layer * width + g * HPG * HD, HPG * HD)] = rows_t.astype(BF16)

    @pl.when(near)
    def _():
        layer_terms(0)

    layer_terms(1)

    @pl.when(me == 0)
    def _():
        @pl.loop(1, PLANE)
        def _(p):
            @pl.when(p < 8)
            def _():
                send(q_units.at[:, pl.ds(q_start(p), 384)], r_q, 2, plane_dev(p))

            @pl.when(p >= 8)
            def _():
                send(q_units.at[:, pl.ds(q_start(p), 256)], r_q.at[:, pl.ds(0, 256)], 2, plane_dev(p))

        r_q[...] = q_units[:, 0:384]

    my_unit = unit_of(pid)
    owns_global = my_unit >= 8

    @pl.loop(1, PLANE)
    def _(k):
        p = (pid + k) % PLANE
        u = unit_of(p)

        @pl.when(jnp.logical_or(near, u >= 8))
        def _():
            send(part.at[u], r_kv.at[pid], 3, plane_dev(p))

    @pl.when(jnp.logical_or(near, owns_global))
    def _():
        r_kv[pid] = part[my_unit]

    rw_kv[pid] = w_kv[:, pl.ds(pl.multiple_of(my_unit * HD, HD), HD)]

    @pl.when(wide)
    def _():
        rw_q[pid] = w_q[:, pl.ds(q_start(pid), 384)]
        wait_recv(rw_q.at[pl.ds(0, PLANE - 1)], 1)
        wp[:, 0:20, 128:512] = rw_q[...]

    @pl.when(jnp.logical_not(wide))
    def _():
        rw_q[pid, :, 0:256] = w_q[:, pl.ds(q_start(pid), 256)]
        wait_recv(rw_q.at[pl.ds(0, PLANE - 1), :, pl.ds(0, 256)], 1)
        wp[:, 0:20, 128:384] = rw_q[:, :, 0:256]

    wait_recv(rw_kv.at[pl.ds(0, PLANE - 1)], 0)
    wp[:, 0:20, 0:128] = rw_kv[...]

    @pl.when(owns_global)
    def _():
        wait_recv(r_kv.at[pl.ds(0, PLANE - 1)], 3)
        acc = r_kv[0].astype(F32)
        for n in range(1, PLANE):
            acc = acc + r_kv[n].astype(F32)
        s_buf[...] = acc

    @pl.when(jnp.logical_not(owns_global))
    def _():
        @pl.when(near)
        def _():
            wait_recv(r_kv.at[pl.ds(0, 3)], 3)

        @pl.when(jnp.logical_not(near))
        def _():
            wait_recv(r_kv.at[pl.ds(0, 4)], 3)

        acc = r_kv[0].astype(F32)
        for n in range(1, 4):
            acc = acc + r_kv[n].astype(F32)
        s_buf[...] = acc

    @pl.loop(1, zs)
    def _(k):
        zz = (z + k) % zs
        send(s_buf.at[pl.ds(pl.multiple_of(8 * zz, 8), 8)], r_z.at[z], 4, z_dev(zz))

    r_z[z] = s_buf[pl.ds(pl.multiple_of(8 * z, 8), 8), :]

    @pl.when(z == 0)
    def _():
        @pl.when(wide)
        def _():
            @pl.when(pid != 0)
            def _():
                wait_recv(r_q, 2)

            @pl.loop(1, zs)
            def _(zz):
                send(
                    r_q.at[pl.ds(pl.multiple_of(8 * zz, 8), 8)],
                    g_buf.at[zz, :, pl.ds(128, 384)], 5, z_dev(zz),
                )

            g_buf[0, :, 128:512] = r_q[0:8, :]

        @pl.when(jnp.logical_not(wide))
        def _():
            wait_recv(r_q.at[:, pl.ds(0, 256)], 2)

            @pl.loop(1, zs)
            def _(zz):
                send(
                    r_q.at[pl.ds(pl.multiple_of(8 * zz, 8), 8), pl.ds(0, 256)],
                    g_buf.at[zz, :, pl.ds(128, 256)], 5, z_dev(zz),
                )

            g_buf[0, :, 128:384] = r_q[0:8, 0:256]

    wait_recv(r_z.at[pl.ds(0, zs - 1)], 4)
    g_buf[z, :, 0:128] = jnp.sum(r_z[...], axis=0).astype(BF16)

    @pl.when(wide)
    def _():
        @pl.when(z != 0)
        def _():
            wait_recv(g_buf.at[0, :, pl.ds(128, 384)], 5)

        @pl.loop(1, zs)
        def _(k):
            send(g_buf.at[z], g_buf.at[z], 6, z_dev((z + k) % zs))

        wait_recv(g_buf.at[pl.ds(0, zs - 1)], 6)

    @pl.when(jnp.logical_not(wide))
    def _():
        @pl.when(z != 0)
        def _():
            wait_recv(g_buf.at[0, :, pl.ds(128, 256)], 5)

        @pl.loop(1, zs)
        def _(k):
            send(
                g_buf.at[z, :, pl.ds(0, 384)], g_buf.at[z, :, pl.ds(0, 384)], 6, z_dev((z + k) % zs)
            )

        wait_recv(g_buf.at[pl.ds(0, zs - 1), :, pl.ds(0, 384)], 6)

    g_kv = g_buf[:, :, 0:128].reshape(HD, HD)
    w_rows = wp[...].reshape(PLANE * 32, 512)
    total = nt(w_rows[:, 0:128], g_kv)
    for slot in range(3):
        cut = slice(128 * (slot + 1), 128 * (slot + 2))
        total = total + nn(w_rows[:, cut], g_buf[:, :, cut].reshape(HD, HD))
    o_send[...] = total.reshape(PLANE, 32, HD)

    @pl.loop(1, PLANE)
    def _(k):
        p = (pid + k) % PLANE
        send(o_send.at[p, pl.ds(0, 24)], r_o.at[pid], 7, plane_dev(p))

    r_o[pid] = o_send[pid, 0:24, :]
    wait_recv(r_o.at[pl.ds(0, PLANE - 1)], 7)
    half[...] = jnp.sum(r_o[...], axis=0)
    last = pltpu.make_async_remote_copy(
        src_ref=half, dst_ref=r_half, send_sem=send_sem.at[8], recv_sem=recv_sem.at[8],
        device_id=(me, 1 - kv), device_id_type=MESH,
    )
    last.start()

    wait_send(rw_kv.at[pl.ds(0, PLANE - 1)], 0)

    @pl.when(wide)
    def _():
        wait_send(rw_q.at[pl.ds(0, 7)], 1)
        wait_send(rw_q.at[pl.ds(0, 8), :, pl.ds(0, 256)], 1)
        wait_send(g_buf.at[pl.ds(0, zs - 1)], 6)

    @pl.when(jnp.logical_not(wide))
    def _():
        wait_send(rw_q.at[pl.ds(0, 8)], 1)
        wait_send(rw_q.at[pl.ds(0, 7), :, pl.ds(0, 256)], 1)
        wait_send(g_buf.at[pl.ds(0, zs - 1), :, pl.ds(0, 384)], 6)

    @pl.when(me == 0)
    def _():
        wait_send(q_units.at[:, pl.ds(0, 7 * 384 + 8 * 256)], 2)

    @pl.when(near)
    def _():
        wait_send(part.at[pl.ds(0, PLANE - 1)], 3)

    @pl.when(jnp.logical_and(jnp.logical_not(near), owns_global))
    def _():
        wait_send(part.at[pl.ds(0, 7)], 3)

    @pl.when(jnp.logical_and(jnp.logical_not(near), jnp.logical_not(owns_global)))
    def _():
        wait_send(part.at[pl.ds(0, 8)], 3)

    wait_send(r_z.at[pl.ds(0, zs - 1)], 4)

    @pl.when(jnp.logical_and(z == 0, wide))
    def _():
        wait_send(g_buf.at[pl.ds(0, zs - 1), :, pl.ds(128, 384)], 5)

    @pl.when(jnp.logical_and(z == 0, jnp.logical_not(wide)))
    def _():
        wait_send(g_buf.at[pl.ds(0, zs - 1), :, pl.ds(128, 256)], 5)

    wait_send(r_o.at[pl.ds(0, PLANE - 1)], 7)
    last.wait()
    both = half[...] + r_half[...]
    full = jnp.concatenate([both, jnp.zeros((HD - 24, HD), F32)], axis=0)
    o_ref[...] = jnp.transpose(full)[:, 0:20]


def solution(mesh):
    zs = mesh.shape["ctx"] // PLANE

    def local(*args):
        tokens, width = args[0].shape
        prompt, keys = args[4].shape
        cols = args[12].shape[0]
        heads = args[3].shape[1]
        any_spec = pl.BlockSpec(memory_space=pl.ANY)
        return pl.pallas_call(
            functools.partial(body, zs),
            out_shape=jax.ShapeDtypeStruct((prompt, cols), F32),
            in_specs=[any_spec] * 18,
            out_specs=pl.BlockSpec(memory_space=pltpu.VMEM),
            scratch_shapes=[
                pltpu.VMEM((2, tokens, width), BF16),
                pltpu.VMEM((2, tokens, width), BF16),
                pltpu.VMEM((2, tokens, width), BF16),
                pltpu.VMEM((2, tokens, heads), F32),
                pltpu.VMEM((2, HD, tokens), F32),
                pltpu.VMEM((2, prompt, keys), BF16),
                pltpu.VMEM((2, prompt, keys), BF16),
                pltpu.VMEM((cols, 4 * keys), BF16),
                pltpu.VMEM((cols, 2 * width), BF16),
                pltpu.VMEM((PLANE, cols, HD), BF16),
                pltpu.VMEM((PLANE, cols, 3 * HD), BF16),
                pltpu.VMEM((PLANE, 32, 4 * HD), BF16),
                pltpu.VMEM((PLANE, HD, HD), BF16),
                pltpu.VMEM((PLANE, HD, HD), BF16),
                pltpu.VMEM((HD, HD), F32),
                pltpu.VMEM((zs, 8, HD), F32),
                pltpu.VMEM((HD, 2 * width), BF16),
                pltpu.VMEM((HD, 3 * HD), BF16),
                pltpu.VMEM((zs, 8, 4 * HD), BF16),
                pltpu.VMEM((PLANE, 32, HD), F32),
                pltpu.VMEM((PLANE, 24, HD), F32),
                pltpu.VMEM((24, HD), F32),
                pltpu.VMEM((24, HD), F32),
                pltpu.SemaphoreType.DMA((18,)),
                pltpu.SemaphoreType.DMA((9,)),
                pltpu.SemaphoreType.DMA((9,)),
            ],
            compiler_params=pltpu.CompilerParams(
                collective_id=0, has_side_effects=True, vmem_limit_bytes=48 * 1024 * 1024
            ),
            name="prompt_grad",
        )(*args)

    split = P("ctx", "kv")
    keys = P(None, "kv")
    layer = (split, split, split, split, keys, keys)
    return jax.shard_map(
        local,
        mesh=mesh,
        in_specs=layer + layer + (split,) * 6,
        out_specs=P(None, "ctx"),
        check_vma=False,
    )
```

time: 1450 us -> 87.3 us (0.06)
  blocking collectives: 1410 us -> 0 us
  Pallas kernels: 0 us -> 70.9 us
  local copies, waits for them, and re-layouts: 33.8 us -> 15.6 us
    psum x2 -> x0, blocking collectives: 1410 us -> none  [the longest x1 1190 us: local(): lax.psum((place_rows(stretch_terms[0], offset, prompt_len), place_rows(gl...]
    pallas_call x0 -> x1, Pallas kernels: none -> 70.9 us  [local(): pl.pallas_call(functools.partial(body, zs), out_shape=jax.ShapeDtypeStruc...]
    dynamic_update_slice x2 -> x0, local copies, waits for them, and re-layouts: 21.1 us -> none  [place_rows(): lax.dynamic_update_slice(padded, rows, (jnp.minimum(offset, prompt_len), 0))]
where the time goes in v1:
time: 87.3 us; the launch traced here: 86.6 us
  Pallas kernels  70.9 us (81%)
  local copies, waits for them, and re-layouts  15.6 us (18%)
    pallas_call x1, Pallas kernels, local(): pl.pallas_call(functools.partial(body, zs), out_shape=jax.ShapeDtypeStruc...  70.9 us
    unnamed x34, local copies, waits for them, and re-layouts  14.9 us

profile of v1, /device:TPU:1, one launch (start us, length us, event | category | flops | bytes accessed | tf_op | source)
XLA Modules:
  0.0 86.6 jit_solution(12068381829069292407)
XLA Ops:
  0.0 0.0 copy-start.6
  0.0 0.8 copy.19.slse
  0.8 0.0 copy-start.12
  0.9 0.8 copy.20.glse
  1.7 0.0 copy-done.6
  1.7 0.0 copy-done.12
  1.7 0.0 copy-start
  1.7 1.1 %copy-done = bf16[128,2560]{1,0:T(8,128)(2,1)S(1)} copy-done((bf16[128,2560]{1,0:T(8,128)(2,1)S(1)}, bf16[128,2560]{1,0:T(8,128)(2,1)}, u32[]{:S(2)}) %copy-start) | copy-done | bytes 655384
  2.8 0.0 copy-start.1
  2.8 1.1 %copy-done.1 = bf16[128,2560]{1,0:T(8,128)(2,1)S(1)} copy-done((bf16[128,2560]{1,0:T(8,128)(2,1)S(1)}, bf16[128,2560]{1,0:T(8,128)(2,1)}, u32[]{:S(2)}) %copy-start.1) | copy-done | bytes 655384
  3.9 0.0 copy-start.2
  3.9 1.1 %copy-done.2 = bf16[128,2560]{1,0:T(8,128)(2,1)S(1)} copy-done((bf16[128,2560]{1,0:T(8,128)(2,1)S(1)}, bf16[128,2560]{1,0:T(8,128)(2,1)}, u32[]{:S(2)}) %copy-start.2) | copy-done | bytes 655384
  5.0 0.0 copy-start.3
  5.0 1.1 %copy-done.3 = bf16[128,2560]{1,0:T(8,128)(2,1)S(1)} copy-done((bf16[128,2560]{1,0:T(8,128)(2,1)S(1)}, bf16[128,2560]{1,0:T(8,128)(2,1)}, u32[]{:S(2)}) %copy-start.3) | copy-done | bytes 655384
  6.0 0.0 copy-start.4
  6.0 1.1 %copy-done.4 = bf16[128,2560]{1,0:T(8,128)(2,1)S(1)} copy-done((bf16[128,2560]{1,0:T(8,128)(2,1)S(1)}, bf16[128,2560]{1,0:T(8,128)(2,1)}, u32[]{:S(2)}) %copy-start.4) | copy-done | bytes 655384
  7.1 0.0 copy-start.5
  7.1 1.1 %copy-done.5 = bf16[128,2560]{1,0:T(8,128)(2,1)S(1)} copy-done((bf16[128,2560]{1,0:T(8,128)(2,1)S(1)}, bf16[128,2560]{1,0:T(8,128)(2,1)}, u32[]{:S(2)}) %copy-start.5) | copy-done | bytes 655384
  8.2 0.0 copy-start.7
  8.2 0.9 %copy-done.7 = bf16[128,512]{1,0:T(8,128)(2,1)S(1)} copy-done((bf16[128,512]{1,0:T(8,128)(2,1)S(1)}, bf16[128,512]{1,0:T(8,128)(2,1)}, u32[]{:S(2)}) %copy-start.7) | copy-done | bytes 131096
  9.1 0.0 copy-start.8
  9.1 0.9 %copy-done.8 = bf16[128,512]{1,0:T(8,128)(2,1)S(1)} copy-done((bf16[128,512]{1,0:T(8,128)(2,1)S(1)}, bf16[128,512]{1,0:T(8,128)(2,1)}, u32[]{:S(2)}) %copy-start.8) | copy-done | bytes 131096
  10.0 0.0 copy-start.9
  10.0 0.9 %copy-done.9 = bf16[128,512]{1,0:T(8,128)(2,1)S(1)} copy-done((bf16[128,512]{1,0:T(8,128)(2,1)S(1)}, bf16[128,512]{1,0:T(8,128)(2,1)}, u32[]{:S(2)}) %copy-start.9) | copy-done | bytes 131096
  10.9 0.0 copy-start.10
  10.9 0.9 %copy-done.10 = bf16[20,2560]{1,0:T(8,128)(2,1)S(1)} copy-done((bf16[20,2560]{1,0:T(8,128)(2,1)S(1)}, bf16[20,2560]{1,0:T(8,128)(2,1)}, u32[]{:S(2)}) %copy-start.10) | copy-done | bytes 102424
  11.8 0.0 copy-start.11
  11.8 0.9 %copy-done.11 = bf16[20,2560]{1,0:T(8,128)(2,1)S(1)} copy-done((bf16[20,2560]{1,0:T(8,128)(2,1)S(1)}, bf16[20,2560]{1,0:T(8,128)(2,1)}, u32[]{:S(2)}) %copy-start.11) | copy-done | bytes 102424
  12.7 0.0 copy-start.13
  12.7 0.7 copy-done.13
  13.5 0.0 copy-start.14
  13.5 0.7 copy-done.14
  14.2 0.0 copy-start.15
  14.2 0.7 copy-done.15
  14.9 70.9 %prompt_grad.1 = f32[128,20]{1,0:T(8,128)S(1)} custom-call(bf16[128,2560]{1,0:T(8,128)(2,1)S(1)} %copy-done, bf16[128,2560]{1,0:T(8,128)(2,1)S(1)} %copy-done.1, bf16[128,2560]{1,0:T(8,128)(2,1)S(1)} %copy-done.2, f32[128,20]{1,0:T(8,128)S(1)} %copy.19.slse, bf16[128,512]{1,0:T(8,128)(2,1)S(1)} %copy-done.6, bf16[128,512]{1,0:T(8,128)(2,1)S(1)} %copy-done.7, ...), custom_call_target="tpu_custom_call" | custom-call | tf_op jit(solution)/shard_map/prompt_grad/pallas_call | solution.py:398
  85.9 0.7 copy.21
Async XLA Ops:
  0.0 1.7 %copy-start.6 = (bf16[128,512]{1,0:T(8,128)(2,1)S(1)}, bf16[128,512]{1,0:T(8,128)(2,1)}, u32[]{:S(2)}) copy-start(bf16[128,512]{1,0:T(8,128)(2,1)} %spk.1) | copy-start | bytes 393220
  0.8 0.8 copy-start.12
  1.7 1.1 %copy-start = (bf16[128,2560]{1,0:T(8,128)(2,1)S(1)}, bf16[128,2560]{1,0:T(8,128)(2,1)}, u32[]{:S(2)}) copy-start(bf16[128,2560]{1,0:T(8,128)(2,1)} %sq.1) | copy-start | bytes 1966084
  2.8 1.1 %copy-start.1 = (bf16[128,2560]{1,0:T(8,128)(2,1)S(1)}, bf16[128,2560]{1,0:T(8,128)(2,1)}, u32[]{:S(2)}) copy-start(bf16[128,2560]{1,0:T(8,128)(2,1)} %sdo.1) | copy-start | bytes 1966084
  3.9 1.1 %copy-start.2 = (bf16[128,2560]{1,0:T(8,128)(2,1)S(1)}, bf16[128,2560]{1,0:T(8,128)(2,1)}, u32[]{:S(2)}) copy-start(bf16[128,2560]{1,0:T(8,128)(2,1)} %sout.1) | copy-start | bytes 1966084
  5.0 1.1 %copy-start.3 = (bf16[128,2560]{1,0:T(8,128)(2,1)S(1)}, bf16[128,2560]{1,0:T(8,128)(2,1)}, u32[]{:S(2)}) copy-start(bf16[128,2560]{1,0:T(8,128)(2,1)} %gq.1) | copy-start | bytes 1966084
  6.0 1.1 %copy-start.4 = (bf16[128,2560]{1,0:T(8,128)(2,1)S(1)}, bf16[128,2560]{1,0:T(8,128)(2,1)}, u32[]{:S(2)}) copy-start(bf16[128,2560]{1,0:T(8,128)(2,1)} %gdo.1) | copy-start | bytes 1966084
  7.1 1.1 %copy-start.5 = (bf16[128,2560]{1,0:T(8,128)(2,1)S(1)}, bf16[128,2560]{1,0:T(8,128)(2,1)}, u32[]{:S(2)}) copy-start(bf16[128,2560]{1,0:T(8,128)(2,1)} %gout.1) | copy-start | bytes 1966084
  8.2 0.9 %copy-start.7 = (bf16[128,512]{1,0:T(8,128)(2,1)S(1)}, bf16[128,512]{1,0:T(8,128)(2,1)}, u32[]{:S(2)}) copy-start(bf16[128,512]{1,0:T(8,128)(2,1)} %spv.1) | copy-start | bytes 393220
  9.1 0.9 %copy-start.8 = (bf16[128,512]{1,0:T(8,128)(2,1)S(1)}, bf16[128,512]{1,0:T(8,128)(2,1)}, u32[]{:S(2)}) copy-start(bf16[128,512]{1,0:T(8,128)(2,1)} %gpk.1) | copy-start | bytes 393220
  10.0 0.9 %copy-start.9 = (bf16[128,512]{1,0:T(8,128)(2,1)S(1)}, bf16[128,512]{1,0:T(8,128)(2,1)}, u32[]{:S(2)}) copy-start(bf16[128,512]{1,0:T(8,128)(2,1)} %gpv.1) | copy-start | bytes 393220
  10.9 0.9 %copy-start.10 = (bf16[20,2560]{1,0:T(8,128)(2,1)S(1)}, bf16[20,2560]{1,0:T(8,128)(2,1)}, u32[]{:S(2)}) copy-start(bf16[20,2560]{1,0:T(8,128)(2,1)} %wqs.1) | copy-start | bytes 307204
  11.8 0.9 %copy-start.11 = (bf16[20,2560]{1,0:T(8,128)(2,1)S(1)}, bf16[20,2560]{1,0:T(8,128)(2,1)}, u32[]{:S(2)}) copy-start(bf16[20,2560]{1,0:T(8,128)(2,1)} %wqg.1) | copy-start | bytes 307204
  12.7 0.7 copy-start.13
  13.5 0.7 copy-start.14
  14.2 0.7 copy-start.15

commit v2 on v1

v2 whole, which is shorter than its diff:
```python
import functools

import jax
import jax.numpy as jnp
from jax import lax
from jax.experimental import pallas as pl
from jax.experimental.pallas import tpu as pltpu
from jax.sharding import PartitionSpec as P

HD = 128
HPG = 5
NEG = -1e30
PLANE = 16
MESH = pl.DeviceIdType.MESH
F32 = jnp.float32
BF16 = jnp.bfloat16


def nt(a, b):
    return lax.dot_general(a, b, (((1,), (1,)), ((), ())), preferred_element_type=F32)


def nn(a, b):
    return lax.dot_general(a, b, (((1,), (0,)), ((), ())), preferred_element_type=F32)


def unit_of(p):
    parity = (p % 4 + p // 4) % 2
    return p // 2 + 8 * (1 - parity)


def pos_of(u):
    return next(p for p in range(PLANE) if unit_of(p) == u)


def pack(ds):
    strips = [ds[16 * s:16 * (s + 1)] for s in range(8)]
    rows = [strips[0]]
    for s in range(1, 4):
        rows.append(strips[s] + pltpu.roll(strips[8 - s], 16 * s, 1))
    rows.append(strips[4])
    return jnp.concatenate(rows, axis=0)


def unpack(packed):
    lane = lax.broadcasted_iota(jnp.int32, (16, HD), 1)
    rows = [packed[16 * s:16 * (s + 1)] for s in range(5)]
    low = [jnp.where(lane >= 16 * s, rows[s], 0.0) for s in range(1, 4)]
    high = [
        jnp.where(lane >= HD - 16 * s, pltpu.roll(rows[s], HD - 16 * s, 1), 0.0) for s in range(3, 0, -1)
    ]
    return jnp.concatenate([rows[0]] + low + [rows[4]] + high, axis=0)


W, SLOT, RS, ZRS, PASS, GATHER, OUT, CORE, FIRST = 0, 1, 4, 5, 6, 7, 8, 9, 10


def body(
    zs,
    sq, sdo, sout, slse, spk, spv,
    gq, gdo, gout, glse, gpk, gpv,
    wqs, wks, wvs, wqg, wkg, wvg,
    o_ref,
    q_buf, do_buf, out_buf, lse_buf, pk_buf, pv_buf,
    w_all, r_w, wp,
    part, r_kv, s_buf, r_z, g_buf,
    units, r_ds, key_t,
    o_send, r_o, half, r_half,
    load_sem, send_sem, recv_sem,
):
    me = lax.axis_index("ctx")
    kv = lax.axis_index("kv")
    pid = me // zs
    z = me % zs
    groups = pk_buf.shape[2] // HD
    heads = groups * HPG
    tokens = q_buf.shape[1]
    inv_root = HD ** (-0.5)
    near = pid < 4
    my_unit = unit_of(pid)
    owns_global = my_unit >= 8
    owns_near = my_unit < 8

    def plane_dev(p):
        return (p * zs + z, kv)

    def z_dev(zz):
        return (pid * zs + zz, kv)

    def send(src, dst, phase, dev, arrive=None):
        pltpu.make_async_remote_copy(
            src_ref=src, dst_ref=dst, send_sem=send_sem.at[phase],
            recv_sem=recv_sem.at[phase if arrive is None else arrive],
            device_id=dev, device_id_type=MESH,
        ).start()

    def wait_recv(ref, phase):
        pltpu.make_async_copy(ref, ref, recv_sem.at[phase]).wait()

    def wait_send(ref, phase):
        pltpu.make_async_copy(ref, ref, send_sem.at[phase]).wait()

    barrier = pltpu.get_barrier_semaphore()

    @pl.loop(0, zs - 1)
    def _(k):
        step = jnp.where(k % 2 == 0, zs // 2 + (k + 1) // 2, zs // 2 - (k + 1) // 2)
        pl.semaphore_signal(barrier, inc=1, device_id=z_dev((z + step) % zs), device_id_type=MESH)

    @pl.loop(1, PLANE)
    def _(k):
        pl.semaphore_signal(barrier, inc=1, device_id=plane_dev((pid + k) % PLANE), device_id_type=MESH)

    pl.semaphore_signal(barrier, inc=1, device_id=(me, 1 - kv), device_id_type=MESH)

    keys = groups * HD
    cut = 2048 - heads * HD
    layer_loads = []
    for layer, srcs in enumerate(((sq, sdo, sout, slse, spv, spk), (gq, gdo, gout, glse, gpv, gpk))):
        dsts = (q_buf, do_buf, out_buf, lse_buf, pv_buf, pk_buf)
        layer_loads.append([
            pltpu.make_async_copy(s, d.at[layer], load_sem.at[8 + 6 * layer + n])
            for n, (s, d) in enumerate(zip(srcs, dsts))
        ])
    w_srcs = (
        (wks, 0, 0, 0, keys), (wvs, 0, 0, keys, keys), (wkg, 0, 0, 2 * keys, keys), (wvg, 0, 0, 3 * keys, keys),
        (wqg, 0, 1, 0, 2048), (wqg, 2048, 2, 0, 512), (wqs, 0, 2, 512, 1536), (wqs, 1536, 3, 0, 1024),
    )
    w_loads = [
        pltpu.make_async_copy(
            src.at[:, pl.ds(first, size)], w_all.at[slot, :, pl.ds(start, size)], load_sem.at[n]
        )
        for n, (src, first, slot, start, size) in enumerate(w_srcs)
    ]
    for c in layer_loads[1]:
        c.start()
    layer_loads[0][5].start()

    @pl.when(near)
    def _():
        for c in layer_loads[0][:5]:
            c.start()

    for c in w_loads:
        c.start()

    wp[...] = jnp.zeros_like(wp)

    rows = lax.broadcasted_iota(jnp.int32, (HD, tokens), 0)
    cols = lax.broadcasted_iota(jnp.int32, (HD, tokens), 1) + me * tokens
    allowed = rows <= cols
    ones = jnp.ones((16, 2 * HD), BF16)

    def group_terms(layer, g):
        spans = [pl.ds((g * HPG + h) * HD, HD) for h in range(HPG)]
        q_cat = jnp.concatenate([q_buf[layer, :, s] for s in spans], axis=0)
        do_cat = jnp.concatenate([do_buf[layer, :, s] for s in spans], axis=0)
        out_cat = jnp.concatenate([out_buf[layer, :, s] for s in spans], axis=0)
        key = pk_buf[layer, :, g * HD:(g + 1) * HD]
        val = pv_buf[layer, :, g * HD:(g + 1) * HD]
        prod = do_cat.astype(F32) * out_cat.astype(F32)
        high = prod.astype(BF16)
        low = (prod - high.astype(F32)).astype(BF16)
        delta = nt(ones, jnp.concatenate([high, low], axis=1))
        scores = nt(key, q_cat)
        grad_prob = nt(val, do_cat)
        p_parts, ds_parts = [], []
        for h in range(HPG):
            span = slice(h * tokens, (h + 1) * tokens)
            row = g * HPG + h
            arg = scores[:, span] * inv_root - lse_buf[layer, row:row + 1, :]
            probs = jnp.exp(jnp.where(allowed, arg, NEG))
            p_parts.append(probs.astype(BF16))
            ds_parts.append((probs * (grad_prob[:, span] - delta[0:1, span])).astype(BF16))
        part[8 * layer + g] = (nn(jnp.concatenate(ds_parts, axis=1), q_cat) * inv_root).astype(BF16)
        part[8 * layer + 4 + g] = nn(jnp.concatenate(p_parts, axis=1), do_cat).astype(BF16)

        @pl.when(me == 0)
        def _():
            for h in range(HPG):
                units[(1 - layer) * heads + g * HPG + h] = pack(ds_parts[h].astype(F32)).astype(BF16)

    def send_units(first, last):
        for n in range(first, last):
            slot, p = n // 16, pos_of(n % 16)
            if p == 0:
                r_ds[slot] = units[n]
            else:
                send(units.at[n], r_ds.at[slot], FIRST, (p * zs, kv), SLOT + slot)

    for c in layer_loads[1]:
        c.wait()
    for g in range(groups):
        group_terms(1, g)

    pl.semaphore_wait(barrier, (PLANE - 1) + (zs - 1) + 1)

    @pl.when(me == 0)
    def _():
        send_units(0, heads)

    @pl.loop(1, PLANE)
    def _(k):
        p = (pid + k) % PLANE
        u = unit_of(p)

        @pl.when(u >= 8)
        def _():
            send(part.at[u], r_kv.at[pid], RS, plane_dev(p))

    layer_loads[0][5].wait()

    @pl.when(near)
    def _():
        for c in layer_loads[0][:5]:
            c.wait()
        for g in range(groups):
            group_terms(0, g)

            @pl.when(me == 0)
            def _():
                send_units(heads + g * HPG, heads + (g + 1) * HPG)

        @pl.loop(1, PLANE)
        def _(k):
            p = (pid + k) % PLANE
            u = unit_of(p)

            @pl.when(u < 8)
            def _():
                send(part.at[u], r_kv.at[pid], RS, plane_dev(p))

    @pl.when(jnp.logical_or(near, owns_global))
    def _():
        r_kv[pid] = part[my_unit]

    for c in w_loads:
        c.wait()

    @pl.when(owns_global)
    def _():
        wait_recv(r_kv.at[pl.ds(0, PLANE - 1)], RS)
        acc = r_kv[0].astype(F32)
        for n in range(1, PLANE):
            acc = acc + r_kv[n].astype(F32)
        s_buf[...] = acc

    @pl.when(owns_near)
    def _():
        @pl.when(near)
        def _():
            wait_recv(r_kv.at[pl.ds(0, 3)], RS)

        @pl.when(jnp.logical_not(near))
        def _():
            wait_recv(r_kv.at[pl.ds(0, 4)], RS)

        acc = r_kv[0].astype(F32)
        for n in range(1, 4):
            acc = acc + r_kv[n].astype(F32)
        s_buf[...] = acc

    @pl.loop(1, zs)
    def _(k):
        zz = (z + k) % zs
        send(s_buf.at[pl.ds(pl.multiple_of(8 * zz, 8), 8)], r_z.at[z], ZRS, z_dev(zz))

    r_z[z] = s_buf[pl.ds(pl.multiple_of(8 * z, 8), 8), :]

    def pass_on(slot):
        @pl.when(pid != 0)
        def _():
            wait_recv(r_ds.at[slot], SLOT + slot)

        @pl.loop(1, zs)
        def _(zz):
            send(r_ds.at[slot], r_ds.at[slot], PASS, z_dev(zz), SLOT + slot)

    @pl.when(z == 0)
    def _():
        pass_on(0)

    @pl.loop(1, PLANE)
    def _(k):
        p = (pid + k) % PLANE
        u = unit_of(p)
        lanes = pl.ds(pl.multiple_of(u * HD, HD), HD)

        @pl.when(u < 8)
        def _():
            send(w_all.at[:, :, lanes], r_w.at[pid], W, plane_dev(p))

        @pl.when(u >= 8)
        def _():
            send(w_all.at[pl.ds(0, 3), :, lanes], r_w.at[pid, pl.ds(0, 3)], W, plane_dev(p))

    @pl.when(z == 0)
    def _():
        pass_on(1)

        @pl.when(owns_near)
        def _():
            pass_on(2)

    def make_key(slot):
        n = 16 * slot + my_unit
        layer = jnp.where(n < heads, 1, 0)
        g = (n % heads) // HPG
        key = pk_buf[layer, :, pl.ds(pl.multiple_of(g * HD, HD), HD)]
        key_t[slot] = jnp.transpose(key.astype(F32)).astype(BF16)

    my_lanes = pl.ds(pl.multiple_of(my_unit * HD, HD), HD)
    for slot in range(3):
        r_w[pid, slot] = w_all[slot, :, my_lanes]
    make_key(0)
    make_key(1)

    @pl.when(owns_near)
    def _():
        r_w[pid, 3] = w_all[3, :, my_lanes]
        make_key(2)

    wait_recv(r_z.at[pl.ds(0, zs - 1)], ZRS)
    g_buf[z] = jnp.sum(r_z[...], axis=0).astype(BF16)

    @pl.loop(1, zs)
    def _(k):
        send(g_buf.at[z], g_buf.at[z], GATHER, z_dev((z + k) % zs))

    @pl.when(owns_near)
    def _():
        wait_recv(r_w.at[pl.ds(0, PLANE - 1)], W)
        wp[:, 0:20, 384:512] = r_w[:, 3]

    @pl.when(owns_global)
    def _():
        wait_recv(r_w.at[pl.ds(0, PLANE - 1), pl.ds(0, 3)], W)

    for slot in range(3):
        wp[:, 0:20, slot * HD:(slot + 1) * HD] = r_w[:, slot]

    def project(slot):
        ds = unpack(r_ds[slot].astype(F32)).astype(BF16)
        grad_q = (nn(key_t[slot], ds) * inv_root).astype(BF16)
        w_rows = wp[:, :, (slot + 1) * HD:(slot + 2) * HD].reshape(PLANE * 32, HD)
        return nn(w_rows, grad_q).reshape(PLANE, 32, HD)

    @pl.when(z != 0)
    def _():
        wait_recv(r_ds.at[0], SLOT)
        wait_recv(r_ds.at[1], SLOT + 1)

    o_send[...] = project(0) + project(1)

    @pl.when(owns_near)
    def _():
        @pl.when(z != 0)
        def _():
            wait_recv(r_ds.at[2], SLOT + 2)

        o_send[...] += project(2)

    wait_recv(g_buf.at[pl.ds(0, zs - 1)], GATHER)
    w_rows = wp[:, :, 0:HD].reshape(PLANE * 32, HD)
    o_send[...] += nt(w_rows, g_buf[...].reshape(HD, HD)).reshape(PLANE, 32, HD)

    @pl.loop(1, PLANE)
    def _(k):
        p = (pid + k) % PLANE
        send(o_send.at[p, pl.ds(0, 24)], r_o.at[pid], OUT, plane_dev(p))

    r_o[pid] = o_send[pid, 0:24, :]
    wait_recv(r_o.at[pl.ds(0, PLANE - 1)], OUT)
    half[...] = jnp.sum(r_o[...], axis=0)
    last = pltpu.make_async_remote_copy(
        src_ref=half, dst_ref=r_half, send_sem=send_sem.at[CORE], recv_sem=recv_sem.at[CORE],
        device_id=(me, 1 - kv), device_id_type=MESH,
    )
    last.start()

    @pl.when(me == 0)
    def _():
        wait_send(units.at[pl.ds(0, 2 * heads - 2)], FIRST)

    @pl.when(near)
    def _():
        wait_send(part.at[pl.ds(0, PLANE - 1)], RS)

    @pl.when(jnp.logical_and(jnp.logical_not(near), owns_global))
    def _():
        wait_send(part.at[pl.ds(0, 7)], RS)

    @pl.when(jnp.logical_and(jnp.logical_not(near), owns_near))
    def _():
        wait_send(part.at[pl.ds(0, 8)], RS)

    wait_send(r_z.at[pl.ds(0, zs - 1)], ZRS)

    @pl.when(z == 0)
    def _():
        for _ in range(2):
            wait_send(units.at[pl.ds(0, zs - 1)], PASS)

        @pl.when(owns_near)
        def _():
            wait_send(units.at[pl.ds(0, zs - 1)], PASS)

    @pl.when(owns_near)
    def _():
        wait_send(r_w.at[pl.ds(0, 7)], W)
        wait_send(r_w.at[pl.ds(0, 8), pl.ds(0, 3)], W)

    @pl.when(owns_global)
    def _():
        wait_send(r_w.at[pl.ds(0, 8)], W)
        wait_send(r_w.at[pl.ds(0, 7), pl.ds(0, 3)], W)

    wait_send(g_buf.at[pl.ds(0, zs - 1)], GATHER)
    wait_send(r_o.at[pl.ds(0, PLANE - 1)], OUT)
    last.wait()
    o_ref[...] = (half[...] + r_half[...])[0:20, :]


def solution(mesh):
    zs = mesh.shape["ctx"] // PLANE

    def local(*args):
        tokens, width = args[0].shape
        prompt, keys = args[4].shape
        cols = args[12].shape[0]
        heads = args[3].shape[1]
        any_spec = pl.BlockSpec(memory_space=pltpu.HBM)
        args = [jnp.transpose(a) if n in (3, 9) else a for n, a in enumerate(args)]
        out = pl.pallas_call(
            functools.partial(body, zs),
            out_shape=jax.ShapeDtypeStruct((cols, prompt), F32),
            in_specs=[any_spec] * 18,
            out_specs=pl.BlockSpec(memory_space=pltpu.VMEM),
            scratch_shapes=[
                pltpu.VMEM((2, tokens, width), BF16),
                pltpu.VMEM((2, tokens, width), BF16),
                pltpu.VMEM((2, tokens, width), BF16),
                pltpu.VMEM((2, heads, tokens), F32),
                pltpu.VMEM((2, prompt, keys), BF16),
                pltpu.VMEM((2, prompt, keys), BF16),
                pltpu.VMEM((4, cols, PLANE * HD), BF16),
                pltpu.VMEM((PLANE, 4, cols, HD), BF16),
                pltpu.VMEM((PLANE, 32, 4 * HD), BF16),
                pltpu.VMEM((PLANE, HD, HD), BF16),
                pltpu.VMEM((PLANE, HD, HD), BF16),
                pltpu.VMEM((HD, HD), F32),
                pltpu.VMEM((zs, 8, HD), F32),
                pltpu.VMEM((zs, 8, HD), BF16),
                pltpu.VMEM((2 * heads, 80, HD), BF16),
                pltpu.VMEM((3, 80, HD), BF16),
                pltpu.VMEM((3, HD, HD), BF16),
                pltpu.VMEM((PLANE, 32, HD), F32),
                pltpu.VMEM((PLANE, 24, HD), F32),
                pltpu.VMEM((24, HD), F32),
                pltpu.VMEM((24, HD), F32),
                pltpu.SemaphoreType.DMA((20,)),
                pltpu.SemaphoreType.DMA((11,)),
                pltpu.SemaphoreType.DMA((11,)),
            ],
            compiler_params=pltpu.CompilerParams(
                collective_id=0, has_side_effects=True, vmem_limit_bytes=60 * 1024 * 1024
            ),
            name="prompt_grad",
        )(*args)
        return jnp.transpose(out)

    split = P("ctx", "kv")
    keys = P(None, "kv")
    layer = (split, split, split, split, keys, keys)
    return jax.shard_map(
        local,
        mesh=mesh,
        in_specs=layer + layer + (split,) * 6,
        out_specs=P(None, "ctx"),
        check_vma=False,
    )
```

time: 87.3 us -> 58.1 us (0.67)
  Pallas kernels: 70.9 us -> 56.6 us
  local copies, waits for them, and re-layouts: 15.6 us -> 1.31 us
    pallas_call x1, Pallas kernels: 70.9 us -> 56.6 us  [local(): pl.pallas_call(functools.partial(body, zs), out_shape=jax.ShapeDtypeStruc...]
    unnamed x34 -> x1, local copies, waits for them, and re-layouts: 14.9 us -> 1.31 us
where the time goes in v2:
time: 58.1 us; the launch traced here: 57.9 us
  Pallas kernels  56.6 us (97%)
  local copies, waits for them, and re-layouts  1.31 us (2%)
    pallas_call x1, Pallas kernels, local(): pl.pallas_call(functools.partial(body, zs), out_shape=jax.ShapeDtypeStruc...  56.6 us
    unnamed x1, local copies, waits for them, and re-layouts  1.31 us

profile of v2, /device:TPU:1, one launch (start us, length us, event | category | flops | bytes accessed | tf_op | source)
XLA Modules:
  0.0 57.9 jit_solution(16205105625855376433)
XLA Ops:
  0.0 56.6 %prompt_grad.1 = f32[20,128]{1,0:T(8,128)} custom-call(bf16[128,2560]{1,0:T(8,128)(2,1)} %sq.1, bf16[128,2560]{1,0:T(8,128)(2,1)} %sdo.1, bf16[128,2560]{1,0:T(8,128)(2,1)} %sout.1, f32[20,128]{1,0:T(8,128)} %bitcast.4, bf16[128,512]{1,0:T(8,128)(2,1)} %spk.1, bf16[128,512]{1,0:T(8,128)(2,1)} %spv.1, bf16[128,2560]{1,0:T(8,128)(2,1)} %gq.1, ...), custom_call_target="tpu_custom_call" | custom-call | tf_op jit(solution)/shard_map/prompt_grad/pallas_call | solution.py:434
  56.6 1.3 %copy.20 = f32[128,20]{0,1:T(8,128)} copy(f32[128,20]{0,1:T(8,128)} %bitcast.3) | data formatting | bytes 20480

commit v3 on v2

--- a/solution.py
+++ b/solution.py
@@ -27,6 +27,15 @@
 def unit_of(p):
     parity = (p % 4 + p // 4) % 2
     return p // 2 + 8 * (1 - parity)
+
+
+OFFSETS = (
+    (2, 2), (2, 1), (1, 2), (2, 3), (3, 2), (1, 1), (3, 3), (1, 3), (3, 1), (2, 0), (0, 2), (1, 0), (0, 1),
+    (3, 0), (0, 3),
+)
+
+
+HEADS = ((0,) * 16, ((4,) * 4 + (12,) * 4) * 2, (12,) * 4 + (4,) * 4)
 
 
 def pos_of(u):
@@ -81,6 +90,16 @@
     owns_global = my_unit >= 8
     owns_near = my_unit < 8
 
+    row, col = pid // 4, pid % 4
+
+    def peers():
+        for dy, dx in OFFSETS:
+            yield ((row + dy) % 4) * 4 + (col + dx) % 4
+
+    def far(k):
+        step = jnp.where(k % 2 == 0, zs // 2 + (k + 1) // 2, zs // 2 - (k + 1) // 2)
+        return (z + step) % zs
+
     def plane_dev(p):
         return (p * zs + z, kv)
 
@@ -100,18 +119,26 @@
     def wait_send(ref, phase):
         pltpu.make_async_copy(ref, ref, send_sem.at[phase]).wait()
 
+    heads_z = (0, jnp.where(my_unit // 4 % 2 == 0, 4, 12), jnp.where(my_unit < 4, 12, 4))
+    heads_me = (
+        z == 0, z == heads_z[1], jnp.logical_and(owns_near, z == heads_z[2]),
+    )
+
     barrier = pltpu.get_barrier_semaphore()
 
     @pl.loop(0, zs - 1)
     def _(k):
-        step = jnp.where(k % 2 == 0, zs // 2 + (k + 1) // 2, zs // 2 - (k + 1) // 2)
-        pl.semaphore_signal(barrier, inc=1, device_id=z_dev((z + step) % zs), device_id_type=MESH)
-
-    @pl.loop(1, PLANE)
-    def _(k):
-        pl.semaphore_signal(barrier, inc=1, device_id=plane_dev((pid + k) % PLANE), device_id_type=MESH)
+        pl.semaphore_signal(barrier, inc=1, device_id=z_dev(far(k)), device_id_type=MESH)
+
+    for p in peers():
+        pl.semaphore_signal(barrier, inc=1, device_id=plane_dev(p), device_id_type=MESH)
 
     pl.semaphore_signal(barrier, inc=1, device_id=(me, 1 - kv), device_id_type=MESH)
+
+    for slot in (1, 2):
+        @pl.when(jnp.logical_and(pid != 0, heads_me[slot]))
+        def _():
+            pl.semaphore_signal(barrier, inc=1, device_id=(0, kv), device_id_type=MESH)
 
     keys = groups * HD
     cut = 2048 - heads * HD
@@ -180,34 +207,21 @@
             for h in range(HPG):
                 units[(1 - layer) * heads + g * HPG + h] = pack(ds_parts[h].astype(F32)).astype(BF16)
 
-    def send_units(first, last):
-        for n in range(first, last):
-            slot, p = n // 16, pos_of(n % 16)
-            if p == 0:
-                r_ds[slot] = units[n]
-            else:
-                send(units.at[n], r_ds.at[slot], FIRST, (p * zs, kv), SLOT + slot)
+    def send_units():
+        for u in range(PLANE):
+            p = pos_of(u)
+            for slot in range(3 if u < 8 else 2):
+                n = 16 * slot + u
+                head = HEADS[slot][u]
+                if p == 0 and head == 0:
+                    r_ds[slot] = units[n]
+                else:
+                    send(units.at[n], r_ds.at[slot], FIRST, (p * zs + head, kv), SLOT + slot)
 
     for c in layer_loads[1]:
         c.wait()
     for g in range(groups):
         group_terms(1, g)
-
-    pl.semaphore_wait(barrier, (PLANE - 1) + (zs - 1) + 1)
-
-    @pl.when(me == 0)
-    def _():
-        send_units(0, heads)
-
-    @pl.loop(1, PLANE)
-    def _(k):
-        p = (pid + k) % PLANE
-        u = unit_of(p)
-
-        @pl.when(u >= 8)
-        def _():
-            send(part.at[u], r_kv.at[pid], RS, plane_dev(p))
-
     layer_loads[0][5].wait()
 
     @pl.when(near)
@@ -217,18 +231,19 @@
         for g in range(groups):
             group_terms(0, g)
 
-            @pl.when(me == 0)
-            def _():
-                send_units(heads + g * HPG, heads + (g + 1) * HPG)
-
-        @pl.loop(1, PLANE)
-        def _(k):
-            p = (pid + k) % PLANE
-            u = unit_of(p)
-
-            @pl.when(u < 8)
-            def _():
-                send(part.at[u], r_kv.at[pid], RS, plane_dev(p))
+    greeted = (PLANE - 1) + (zs - 1) + 1
+    pl.semaphore_wait(barrier, jnp.where(me == 0, greeted + 23, greeted))
+
+    for p in peers():
+        u = unit_of(p)
+
+        @pl.when(jnp.logical_or(near, u >= 8))
+        def _():
+            send(part.at[u], r_kv.at[pid], RS, plane_dev(p))
+
+    @pl.when(me == 0)
+    def _():
+        send_units()
 
     @pl.when(jnp.logical_or(near, owns_global))
     def _():
@@ -260,29 +275,23 @@
             acc = acc + r_kv[n].astype(F32)
         s_buf[...] = acc
 
-    @pl.loop(1, zs)
+    @pl.loop(0, zs - 1)
     def _(k):
-        zz = (z + k) % zs
+        zz = far(k)
         send(s_buf.at[pl.ds(pl.multiple_of(8 * zz, 8), 8)], r_z.at[z], ZRS, z_dev(zz))
 
     r_z[z] = s_buf[pl.ds(pl.multiple_of(8 * z, 8), 8), :]
 
     def pass_on(slot):
-        @pl.when(pid != 0)
+        @pl.when(pid != 0 if slot == 0 else me >= 0)
         def _():
             wait_recv(r_ds.at[slot], SLOT + slot)
 
-        @pl.loop(1, zs)
-        def _(zz):
-            send(r_ds.at[slot], r_ds.at[slot], PASS, z_dev(zz), SLOT + slot)
-
-    @pl.when(z == 0)
-    def _():
-        pass_on(0)
-
-    @pl.loop(1, PLANE)
-    def _(k):
-        p = (pid + k) % PLANE
+        @pl.loop(0, zs - 1)
+        def _(k):
+            send(r_ds.at[slot], r_ds.at[slot], PASS, z_dev(far(k)), SLOT + slot)
+
+    for p in peers():
         u = unit_of(p)
         lanes = pl.ds(pl.multiple_of(u * HD, HD), HD)
 
@@ -294,13 +303,9 @@
         def _():
             send(w_all.at[pl.ds(0, 3), :, lanes], r_w.at[pid, pl.ds(0, 3)], W, plane_dev(p))
 
-    @pl.when(z == 0)
-    def _():
-        pass_on(1)
-
-        @pl.when(owns_near)
-        def _():
-            pass_on(2)
+    @pl.when(heads_me[0])
+    def _():
+        pass_on(0)
 
     def make_key(slot):
         n = 16 * slot + my_unit
@@ -323,9 +328,17 @@
     wait_recv(r_z.at[pl.ds(0, zs - 1)], ZRS)
     g_buf[z] = jnp.sum(r_z[...], axis=0).astype(BF16)
 
-    @pl.loop(1, zs)
+    @pl.loop(0, zs - 1)
     def _(k):
-        send(g_buf.at[z], g_buf.at[z], GATHER, z_dev((z + k) % zs))
+        send(g_buf.at[z], g_buf.at[z], GATHER, z_dev(far(k)))
+
+    @pl.when(heads_me[1])
+    def _():
+        pass_on(1)
+
+    @pl.when(heads_me[2])
+    def _():
+        pass_on(2)
 
     @pl.when(owns_near)
     def _():
@@ -343,18 +356,18 @@
         ds = unpack(r_ds[slot].astype(F32)).astype(BF16)
         grad_q = (nn(key_t[slot], ds) * inv_root).astype(BF16)
         w_rows = wp[:, :, (slot + 1) * HD:(slot + 2) * HD].reshape(PLANE * 32, HD)
-        return nn(w_rows, grad_q).reshape(PLANE, 32, HD)
-
-    @pl.when(z != 0)
-    def _():
-        wait_recv(r_ds.at[0], SLOT)
-        wait_recv(r_ds.at[1], SLOT + 1)
+        return nn(w_rows, grad_q).reshape(PLANE, 32, HD)[:, 0:20]
+
+    for slot in range(2):
+        @pl.when(z != heads_z[slot])
+        def _():
+            wait_recv(r_ds.at[slot], SLOT + slot)
 
     o_send[...] = project(0) + project(1)
 
     @pl.when(owns_near)
     def _():
-        @pl.when(z != 0)
+        @pl.when(z != heads_z[2])
         def _():
             wait_recv(r_ds.at[2], SLOT + 2)
 
@@ -362,14 +375,12 @@
 
     wait_recv(g_buf.at[pl.ds(0, zs - 1)], GATHER)
     w_rows = wp[:, :, 0:HD].reshape(PLANE * 32, HD)
-    o_send[...] += nt(w_rows, g_buf[...].reshape(HD, HD)).reshape(PLANE, 32, HD)
-
-    @pl.loop(1, PLANE)
-    def _(k):
-        p = (pid + k) % PLANE
-        send(o_send.at[p, pl.ds(0, 24)], r_o.at[pid], OUT, plane_dev(p))
-
-    r_o[pid] = o_send[pid, 0:24, :]
+    o_send[...] += nt(w_rows, g_buf[...].reshape(HD, HD)).reshape(PLANE, 32, HD)[:, 0:20]
+
+    for p in peers():
+        send(o_send.at[p], r_o.at[pid], OUT, plane_dev(p))
+
+    r_o[pid] = o_send[pid]
     wait_recv(r_o.at[pl.ds(0, PLANE - 1)], OUT)
     half[...] = jnp.sum(r_o[...], axis=0)
     last = pltpu.make_async_remote_copy(
@@ -380,7 +391,7 @@
 
     @pl.when(me == 0)
     def _():
-        wait_send(units.at[pl.ds(0, 2 * heads - 2)], FIRST)
+        wait_send(units.at[pl.ds(0, 2 * heads - 1)], FIRST)
 
     @pl.when(near)
     def _():
@@ -396,12 +407,8 @@
 
     wait_send(r_z.at[pl.ds(0, zs - 1)], ZRS)
 
-    @pl.when(z == 0)
-    def _():
-        for _ in range(2):
-            wait_send(units.at[pl.ds(0, zs - 1)], PASS)
-
-        @pl.when(owns_near)
+    for slot in range(3):
+        @pl.when(heads_me[slot])
         def _():
             wait_send(units.at[pl.ds(0, zs - 1)], PASS)
 
@@ -418,7 +425,7 @@
     wait_send(g_buf.at[pl.ds(0, zs - 1)], GATHER)
     wait_send(r_o.at[pl.ds(0, PLANE - 1)], OUT)
     last.wait()
-    o_ref[...] = (half[...] + r_half[...])[0:20, :]
+    o_ref[...] = half[...] + r_half[...]
 
 
 def solution(mesh):
@@ -433,7 +440,7 @@
         args = [jnp.transpose(a) if n in (3, 9) else a for n, a in enumerate(args)]
         out = pl.pallas_call(
             functools.partial(body, zs),
-            out_shape=jax.ShapeDtypeStruct((cols, prompt), F32),
+            out_shape=pltpu.VMEM((cols, prompt), F32),
             in_specs=[any_spec] * 18,
             out_specs=pl.BlockSpec(memory_space=pltpu.VMEM),
             scratch_shapes=[
@@ -454,10 +461,10 @@
                 pltpu.VMEM((2 * heads, 80, HD), BF16),
                 pltpu.VMEM((3, 80, HD), BF16),
                 pltpu.VMEM((3, HD, HD), BF16),
-                pltpu.VMEM((PLANE, 32, HD), F32),
-                pltpu.VMEM((PLANE, 24, HD), F32),
-                pltpu.VMEM((24, HD), F32),
-                pltpu.VMEM((24, HD), F32),
+                pltpu.VMEM((PLANE, cols, HD), F32),
+                pltpu.VMEM((PLANE, cols, HD), F32),
+                pltpu.VMEM((cols, HD), F32),
+                pltpu.VMEM((cols, HD), F32),
                 pltpu.SemaphoreType.DMA((20,)),
                 pltpu.SemaphoreType.DMA((11,)),
                 pltpu.SemaphoreType.DMA((11,)),

time: 58.1 us -> 47.8 us (0.82)
  Pallas kernels: 56.6 us -> 47.1 us
  local copies, waits for them, and re-layouts: 1.31 us -> 0.6 us
    pallas_call x1, Pallas kernels: 56.6 us -> 47.1 us  [local(): pl.pallas_call(functools.partial(body, zs), out_shape=pltpu.VMEM((cols, p...]
    unnamed x1, local copies, waits for them, and re-layouts: 1.31 us -> 0.6 us
where the time goes in v3:
time: 47.8 us; the launch traced here: 47.7 us
  Pallas kernels  47.1 us (99%)
  local copies, waits for them, and re-layouts  0.6 us (1%)
    pallas_call x1, Pallas kernels, local(): pl.pallas_call(functools.partial(body, zs), out_shape=pltpu.VMEM((cols, p...  47.1 us

profile of v3, /device:TPU:1, one launch (start us, length us, event | category | flops | bytes accessed | tf_op | source)
XLA Modules:
  0.0 47.7 jit_solution(2311131858305985278)
XLA Ops:
  0.0 47.1 %prompt_grad.1 = f32[20,128]{1,0:T(8,128)S(1)} custom-call(bf16[128,2560]{1,0:T(8,128)(2,1)} %sq.1, bf16[128,2560]{1,0:T(8,128)(2,1)} %sdo.1, bf16[128,2560]{1,0:T(8,128)(2,1)} %sout.1, f32[20,128]{1,0:T(8,128)} %bitcast.4, bf16[128,512]{1,0:T(8,128)(2,1)} %spk.1, bf16[128,512]{1,0:T(8,128)(2,1)} %spv.1, bf16[128,2560]{1,0:T(8,128)(2,1)} %gq.1, ...), custom_call_target="tpu_custom_call" | custom-call | tf_op jit(solution)/shard_map/prompt_grad/pallas_call | solution.py:441
  47.1 0.6 %copy.20 = f32[128,20]{0,1:T(8,128)} copy(f32[128,20]{0,1:T(8,128)S(1)} %bitcast.3) | data formatting | bytes 20480

commit v4 on v3

--- a/solution.py
+++ b/solution.py
@@ -35,7 +35,7 @@
 )
 
 
-HEADS = ((0,) * 16, ((4,) * 4 + (12,) * 4) * 2, (12,) * 4 + (4,) * 4)
+HEADS = ((0,) * 16, ((4,) * 4 + (12,) * 4) * 2, (12, 12, 0, 0, 4, 4, 0, 0))
 
 
 def pos_of(u):
@@ -61,7 +61,7 @@
     return jnp.concatenate([rows[0]] + low + [rows[4]] + high, axis=0)
 
 
-W, SLOT, RS, ZRS, PASS, GATHER, OUT, CORE, FIRST = 0, 1, 4, 5, 6, 7, 8, 9, 10
+W, SLOT, RS, ZRS, PASS, GATHER, OUT, FIRST = 0, 1, 4, 5, 6, 7, 8, 9
 
 
 def body(
@@ -74,13 +74,13 @@
     w_all, r_w, wp,
     part, r_kv, s_buf, r_z, g_buf,
     units, r_ds, key_t,
-    o_send, r_o, half, r_half,
-    load_sem, send_sem, recv_sem,
+    o_acc, o_send, r_o,
+    load_sem, send_sem, recv_sem, ready_sem,
 ):
     me = lax.axis_index("ctx")
     kv = lax.axis_index("kv")
-    pid = me // zs
-    z = me % zs
+    pid = lax.div(me, zs)
+    z = lax.rem(me, zs)
     groups = pk_buf.shape[2] // HD
     heads = groups * HPG
     tokens = q_buf.shape[1]
@@ -90,15 +90,20 @@
     owns_global = my_unit >= 8
     owns_near = my_unit < 8
 
-    row, col = pid // 4, pid % 4
+    row, col = lax.div(pid, 4), lax.rem(pid, 4)
+
+    def wrap(index, size):
+        return jnp.where(index >= size, index - size, index)
 
     def peers():
         for dy, dx in OFFSETS:
-            yield ((row + dy) % 4) * 4 + (col + dx) % 4
-
-    def far(k):
-        step = jnp.where(k % 2 == 0, zs // 2 + (k + 1) // 2, zs // 2 - (k + 1) // 2)
-        return (z + step) % zs
+            yield wrap(row + dy, 4) * 4 + wrap(col + dx, 4)
+
+    def column():
+        for k in range(zs - 1):
+            half_way = zs // 2
+            step = half_way + (k + 1) // 2 if k % 2 == 0 else half_way - (k + 1) // 2
+            yield wrap(z + step, zs)
 
     def plane_dev(p):
         return (p * zs + z, kv)
@@ -119,26 +124,49 @@
     def wait_send(ref, phase):
         pltpu.make_async_copy(ref, ref, send_sem.at[phase]).wait()
 
-    heads_z = (0, jnp.where(my_unit // 4 % 2 == 0, 4, 12), jnp.where(my_unit < 4, 12, 4))
+    heads_z = (
+        0, jnp.where(my_unit // 4 % 2 == 0, 4, 12), jnp.where(my_unit % 4 < 2, jnp.where(my_unit < 4, 12, 4), 0),
+    )
     heads_me = (
         z == 0, z == heads_z[1], jnp.logical_and(owns_near, z == heads_z[2]),
     )
 
     barrier = pltpu.get_barrier_semaphore()
 
-    @pl.loop(0, zs - 1)
-    def _(k):
-        pl.semaphore_signal(barrier, inc=1, device_id=z_dev(far(k)), device_id_type=MESH)
-
-    for p in peers():
-        pl.semaphore_signal(barrier, inc=1, device_id=plane_dev(p), device_id_type=MESH)
-
-    pl.semaphore_signal(barrier, inc=1, device_id=(me, 1 - kv), device_id_type=MESH)
+    def greet(dev):
+        pl.semaphore_signal(barrier, inc=1, device_id=dev, device_id_type=MESH)
+
+    for zz in column():
+        greet((pid * zs + zz, 1))
 
     for slot in (1, 2):
-        @pl.when(jnp.logical_and(pid != 0, heads_me[slot]))
-        def _():
-            pl.semaphore_signal(barrier, inc=1, device_id=(0, kv), device_id_type=MESH)
+        @pl.when(jnp.logical_and(jnp.logical_and(pid != 0, z != 0), heads_me[slot]))
+        def _():
+            greet((0, 1))
+
+    def tell(sem):
+        pl.semaphore_signal(sem, inc=1, device_id=(me, 1 - kv), device_id_type=MESH)
+
+    def plane_ready():
+        @pl.when(kv == 0)
+        def _():
+            pl.semaphore_wait(barrier, 2 * (PLANE - 1) + 1)
+            tell(ready_sem.at[0])
+
+        @pl.when(kv == 1)
+        def _():
+            pl.semaphore_wait(ready_sem.at[0], 1)
+
+    def z_ready():
+        @pl.when(kv == 1)
+        def _():
+            greeted = 2 * (zs - 1) + 1
+            pl.semaphore_wait(barrier, jnp.where(me == 0, greeted + 38, greeted))
+            tell(ready_sem.at[1])
+
+        @pl.when(kv == 0)
+        def _():
+            pl.semaphore_wait(ready_sem.at[1], 1)
 
     keys = groups * HD
     cut = 2048 - heads * HD
@@ -161,6 +189,11 @@
     ]
     for c in layer_loads[1]:
         c.start()
+
+    for p in peers():
+        greet((p * zs + z, 0))
+
+    greet((me, 1 - kv))
     layer_loads[0][5].start()
 
     @pl.when(near)
@@ -207,10 +240,11 @@
             for h in range(HPG):
                 units[(1 - layer) * heads + g * HPG + h] = pack(ds_parts[h].astype(F32)).astype(BF16)
 
-    def send_units():
-        for u in range(PLANE):
-            p = pos_of(u)
-            for slot in range(3 if u < 8 else 2):
+    def send_units(slots):
+        for dy, dx in OFFSETS + ((0, 0),):
+            p = 4 * dy + dx
+            u = unit_of(p)
+            for slot in (t for t in slots if t < 2 or u < 8):
                 n = 16 * slot + u
                 head = HEADS[slot][u]
                 if p == 0 and head == 0:
@@ -222,6 +256,15 @@
         c.wait()
     for g in range(groups):
         group_terms(1, g)
+    plane_ready()
+
+    for p in peers():
+        u = unit_of(p)
+
+        @pl.when(u >= 8)
+        def _():
+            send(part.at[u], r_kv.at[pid], RS, plane_dev(p))
+
     layer_loads[0][5].wait()
 
     @pl.when(near)
@@ -230,20 +273,22 @@
             c.wait()
         for g in range(groups):
             group_terms(0, g)
-
-    greeted = (PLANE - 1) + (zs - 1) + 1
-    pl.semaphore_wait(barrier, jnp.where(me == 0, greeted + 23, greeted))
-
-    for p in peers():
-        u = unit_of(p)
-
-        @pl.when(jnp.logical_or(near, u >= 8))
-        def _():
-            send(part.at[u], r_kv.at[pid], RS, plane_dev(p))
+            for u in (g, 4 + g):
+                p = pos_of(u)
+
+                @pl.when(pid != p)
+                def _():
+                    send(part.at[u], r_kv.at[pid], RS, plane_dev(p))
 
     @pl.when(me == 0)
     def _():
-        send_units()
+        send_units((0,))
+
+    z_ready()
+
+    @pl.when(me == 0)
+    def _():
+        send_units((1, 2))
 
     @pl.when(jnp.logical_or(near, owns_global))
     def _():
@@ -275,9 +320,7 @@
             acc = acc + r_kv[n].astype(F32)
         s_buf[...] = acc
 
-    @pl.loop(0, zs - 1)
-    def _(k):
-        zz = far(k)
+    for zz in column():
         send(s_buf.at[pl.ds(pl.multiple_of(8 * zz, 8), 8)], r_z.at[z], ZRS, z_dev(zz))
 
     r_z[z] = s_buf[pl.ds(pl.multiple_of(8 * z, 8), 8), :]
@@ -287,9 +330,8 @@
         def _():
             wait_recv(r_ds.at[slot], SLOT + slot)
 
-        @pl.loop(0, zs - 1)
-        def _(k):
-            send(r_ds.at[slot], r_ds.at[slot], PASS, z_dev(far(k)), SLOT + slot)
+        for zz in column():
+            send(r_ds.at[slot], r_ds.at[slot], PASS, z_dev(zz), SLOT + slot)
 
     for p in peers():
         u = unit_of(p)
@@ -328,9 +370,8 @@
     wait_recv(r_z.at[pl.ds(0, zs - 1)], ZRS)
     g_buf[z] = jnp.sum(r_z[...], axis=0).astype(BF16)
 
-    @pl.loop(0, zs - 1)
-    def _(k):
-        send(g_buf.at[z], g_buf.at[z], GATHER, z_dev(far(k)))
+    for zz in column():
+        send(g_buf.at[z], g_buf.at[z], GATHER, z_dev(zz))
 
     @pl.when(heads_me[1])
     def _():
@@ -363,7 +404,7 @@
         def _():
             wait_recv(r_ds.at[slot], SLOT + slot)
 
-    o_send[...] = project(0) + project(1)
+    o_acc[...] = project(0) + project(1)
 
     @pl.when(owns_near)
     def _():
@@ -371,23 +412,19 @@
         def _():
             wait_recv(r_ds.at[2], SLOT + 2)
 
-        o_send[...] += project(2)
+        o_acc[...] += project(2)
 
     wait_recv(g_buf.at[pl.ds(0, zs - 1)], GATHER)
     w_rows = wp[:, :, 0:HD].reshape(PLANE * 32, HD)
-    o_send[...] += nt(w_rows, g_buf[...].reshape(HD, HD)).reshape(PLANE, 32, HD)[:, 0:20]
-
+    last_term = nt(w_rows, g_buf[...].reshape(HD, HD)).reshape(PLANE, 32, HD)[:, 0:20]
+    o_send[...] = (o_acc[...] + last_term).astype(o_send.dtype)
+
+    mine = PLANE * kv + pid
     for p in peers():
-        send(o_send.at[p], r_o.at[pid], OUT, plane_dev(p))
-
-    r_o[pid] = o_send[pid]
-    wait_recv(r_o.at[pl.ds(0, PLANE - 1)], OUT)
-    half[...] = jnp.sum(r_o[...], axis=0)
-    last = pltpu.make_async_remote_copy(
-        src_ref=half, dst_ref=r_half, send_sem=send_sem.at[CORE], recv_sem=recv_sem.at[CORE],
-        device_id=(me, 1 - kv), device_id_type=MESH,
-    )
-    last.start()
+        for core in range(2):
+            send(o_send.at[p], r_o.at[mine], OUT, (p * zs + z, core))
+    send(o_send.at[pid], r_o.at[mine], OUT, (me, 1 - kv))
+    r_o[mine] = o_send[pid]
 
     @pl.when(me == 0)
     def _():
@@ -423,9 +460,9 @@
         wait_send(r_w.at[pl.ds(0, 7), pl.ds(0, 3)], W)
 
     wait_send(g_buf.at[pl.ds(0, zs - 1)], GATHER)
-    wait_send(r_o.at[pl.ds(0, PLANE - 1)], OUT)
-    last.wait()
-    o_ref[...] = half[...] + r_half[...]
+    wait_send(r_o.at[pl.ds(0, 2 * PLANE - 1)], OUT)
+    wait_recv(r_o.at[pl.ds(0, 2 * PLANE - 1)], OUT)
+    o_ref[...] = jnp.sum(r_o[...].astype(F32), axis=0)
 
 
 def solution(mesh):
@@ -463,11 +500,11 @@
                 pltpu.VMEM((3, HD, HD), BF16),
                 pltpu.VMEM((PLANE, cols, HD), F32),
                 pltpu.VMEM((PLANE, cols, HD), F32),
-                pltpu.VMEM((cols, HD), F32),
-                pltpu.VMEM((cols, HD), F32),
+                pltpu.VMEM((2 * PLANE, cols, HD), F32),
                 pltpu.SemaphoreType.DMA((20,)),
-                pltpu.SemaphoreType.DMA((11,)),
-                pltpu.SemaphoreType.DMA((11,)),
+                pltpu.SemaphoreType.DMA((10,)),
+                pltpu.SemaphoreType.DMA((10,)),
+                pltpu.SemaphoreType.REGULAR((2,)),
             ],
             compiler_params=pltpu.CompilerParams(
                 collective_id=0, has_side_effects=True, vmem_limit_bytes=60 * 1024 * 1024

time: 47.8 us -> 46.1 us (0.964)
  Pallas kernels: 47.1 us -> 45.3 us
    pallas_call x1, Pallas kernels: 47.1 us -> 45.3 us  [local(): pl.pallas_call(functools.partial(body, zs), out_shape=pltpu.VMEM((cols, p...]
where the time goes in v4:
time: 46.1 us; the launch traced here: 45.9 us
  Pallas kernels  45.3 us (98%)
  local copies, waits for them, and re-layouts  0.6 us (1%)
    pallas_call x1, Pallas kernels, local(): pl.pallas_call(functools.partial(body, zs), out_shape=pltpu.VMEM((cols, p...  45.3 us

profile of v4, /device:TPU:1, one launch (start us, length us, event | category | flops | bytes accessed | tf_op | source)
XLA Modules:
  0.0 45.9 jit_solution(17495353653639544685)
XLA Ops:
  0.0 45.3 %prompt_grad.1 = f32[20,128]{1,0:T(8,128)S(1)} custom-call(bf16[128,2560]{1,0:T(8,128)(2,1)} %sq.1, bf16[128,2560]{1,0:T(8,128)(2,1)} %sdo.1, bf16[128,2560]{1,0:T(8,128)(2,1)} %sout.1, f32[20,128]{1,0:T(8,128)} %bitcast.4, bf16[128,512]{1,0:T(8,128)(2,1)} %spk.1, bf16[128,512]{1,0:T(8,128)(2,1)} %spv.1, bf16[128,2560]{1,0:T(8,128)(2,1)} %gq.1, ...), custom_call_target="tpu_custom_call" | custom-call | tf_op jit(solution)/shard_map/prompt_grad/pallas_call | solution.py:478
  45.3 0.6 %copy.20 = f32[128,20]{0,1:T(8,128)} copy(f32[128,20]{0,1:T(8,128)S(1)} %bitcast.3) | data formatting | bytes 20480

commit v5 on v4

--- a/solution.py
+++ b/solution.py
@@ -42,23 +42,29 @@
     return next(p for p in range(PLANE) if unit_of(p) == u)
 
 
+STRIP = 8
+HALF = HD // STRIP // 2
+PACKED = STRIP * (HALF + 1)
+
+
 def pack(ds):
-    strips = [ds[16 * s:16 * (s + 1)] for s in range(8)]
+    strips = [ds[STRIP * s:STRIP * (s + 1)] for s in range(2 * HALF)]
     rows = [strips[0]]
-    for s in range(1, 4):
-        rows.append(strips[s] + pltpu.roll(strips[8 - s], 16 * s, 1))
-    rows.append(strips[4])
+    for s in range(1, HALF):
+        rows.append(strips[s] + pltpu.roll(strips[2 * HALF - s], STRIP * s, 1))
+    rows.append(strips[HALF])
     return jnp.concatenate(rows, axis=0)
 
 
 def unpack(packed):
-    lane = lax.broadcasted_iota(jnp.int32, (16, HD), 1)
-    rows = [packed[16 * s:16 * (s + 1)] for s in range(5)]
-    low = [jnp.where(lane >= 16 * s, rows[s], 0.0) for s in range(1, 4)]
+    lane = lax.broadcasted_iota(jnp.int32, (STRIP, HD), 1)
+    rows = [packed[STRIP * s:STRIP * (s + 1)] for s in range(HALF + 1)]
+    low = [jnp.where(lane >= STRIP * s, rows[s], 0.0) for s in range(1, HALF)]
     high = [
-        jnp.where(lane >= HD - 16 * s, pltpu.roll(rows[s], HD - 16 * s, 1), 0.0) for s in range(3, 0, -1)
+        jnp.where(lane >= HD - STRIP * s, pltpu.roll(rows[s], HD - STRIP * s, 1), 0.0)
+        for s in range(HALF - 1, 0, -1)
     ]
-    return jnp.concatenate([rows[0]] + low + [rows[4]] + high, axis=0)
+    return jnp.concatenate([rows[0]] + low + [rows[HALF]] + high, axis=0)
 
 
 W, SLOT, RS, ZRS, PASS, GATHER, OUT, FIRST = 0, 1, 4, 5, 6, 7, 8, 9
@@ -265,6 +271,10 @@
         def _():
             send(part.at[u], r_kv.at[pid], RS, plane_dev(p))
 
+    @pl.when(me == 0)
+    def _():
+        send_units((0,))
+
     layer_loads[0][5].wait()
 
     @pl.when(near)
@@ -280,10 +290,6 @@
                 def _():
                     send(part.at[u], r_kv.at[pid], RS, plane_dev(p))
 
-    @pl.when(me == 0)
-    def _():
-        send_units((0,))
-
     z_ready()
 
     @pl.when(me == 0)
@@ -333,6 +339,10 @@
         for zz in column():
             send(r_ds.at[slot], r_ds.at[slot], PASS, z_dev(zz), SLOT + slot)
 
+    @pl.when(heads_me[0])
+    def _():
+        pass_on(0)
+
     for p in peers():
         u = unit_of(p)
         lanes = pl.ds(pl.multiple_of(u * HD, HD), HD)
@@ -344,10 +354,6 @@
         @pl.when(u >= 8)
         def _():
             send(w_all.at[pl.ds(0, 3), :, lanes], r_w.at[pid, pl.ds(0, 3)], W, plane_dev(p))
-
-    @pl.when(heads_me[0])
-    def _():
-        pass_on(0)
 
     def make_key(slot):
         n = 16 * slot + my_unit
@@ -495,8 +501,8 @@
                 pltpu.VMEM((HD, HD), F32),
                 pltpu.VMEM((zs, 8, HD), F32),
                 pltpu.VMEM((zs, 8, HD), BF16),
-                pltpu.VMEM((2 * heads, 80, HD), BF16),
-                pltpu.VMEM((3, 80, HD), BF16),
+                pltpu.VMEM((2 * heads, PACKED, HD), BF16),
+                pltpu.VMEM((3, PACKED, HD), BF16),
                 pltpu.VMEM((3, HD, HD), BF16),
                 pltpu.VMEM((PLANE, cols, HD), F32),
                 pltpu.VMEM((PLANE, cols, HD), F32),

time: 46.1 us -> 45.6 us (0.989)
  Pallas kernels: 45.3 us -> 44.8 us
    pallas_call x1, Pallas kernels: 45.3 us -> 44.8 us  [local(): pl.pallas_call(functools.partial(body, zs), out_shape=pltpu.VMEM((cols, p...]
where the time goes in v5:
time: 45.6 us; the launch traced here: 45.4 us
  Pallas kernels  44.8 us (98%)
  local copies, waits for them, and re-layouts  0.6 us (1%)
    pallas_call x1, Pallas kernels, local(): pl.pallas_call(functools.partial(body, zs), out_shape=pltpu.VMEM((cols, p...  44.8 us

profile of v5, /device:TPU:1, one launch (start us, length us, event | category | flops | bytes accessed | tf_op | source)
XLA Modules:
  0.0 45.4 jit_solution(13729369256674513026)
XLA Ops:
  0.0 44.8 %prompt_grad.1 = f32[20,128]{1,0:T(8,128)S(1)} custom-call(bf16[128,2560]{1,0:T(8,128)(2,1)} %sq.1, bf16[128,2560]{1,0:T(8,128)(2,1)} %sdo.1, bf16[128,2560]{1,0:T(8,128)(2,1)} %sout.1, f32[20,128]{1,0:T(8,128)} %bitcast.4, bf16[128,512]{1,0:T(8,128)(2,1)} %spk.1, bf16[128,512]{1,0:T(8,128)(2,1)} %spv.1, bf16[128,2560]{1,0:T(8,128)(2,1)} %gq.1, ...), custom_call_target="tpu_custom_call" | custom-call | tf_op jit(solution)/shard_map/prompt_grad/pallas_call | solution.py:484
  44.8 0.6 %copy.20 = f32[128,20]{0,1:T(8,128)} copy(f32[128,20]{0,1:T(8,128)S(1)} %bitcast.3) | data formatting | bytes 20480
